TPU v7x, 512 devices: a whole 4x4x16 slice. The times are simulated.
512 devices in a mesh: seq: 16 (over y, x), mp: 32 (over z, core).
Axes of the slice: x: 4, y: 4, z: 16, core: 2. Of those that a mesh axis runs over, the one named last changes fastest.
Arguments:
- q_proj: bfloat16 [4096, 8192], P('seq', 'mp'), may hold values from -6 to 6
- k_proj: bfloat16 [4096, 8192], P('seq', 'mp'), may hold values from -6 to 6
- v_proj: bfloat16 [4096, 8192], P('seq', 'mp'), may hold values from -6 to 6
- out_grad: bfloat16 [4096, 8192], P('seq', 'mp'), may hold values from -0.75 to 0.75
- out_weight: bfloat16 [8192, 8192], P('mp', 'seq'), may hold values from -0.0625 to 0.0625
- taps: float32 [7, 512], P(None, 'mp'), may hold values from -2.4 to 2.4
Outputs:
- grad_q: bfloat16 [4096, 8192], P('seq', 'mp')
- grad_k: bfloat16 [4096, 8192], P('seq', 'mp')
- grad_v: bfloat16 [4096, 8192], P('seq', 'mp')
- grad_weight: float32 [8192, 8192], P('mp', 'seq')
- grad_taps: float32 [7, 512], P(None, 'mp')
All inputs are finite; a program needn't handle non-finite values.
Results may differ from a plain program's by a relative error of at most 0.0029.
Values may be sent and summed in bfloat16 or wider, within the bound.
A program may use at most 64 MiB of HBM per device.

v0:
```python
import jax
import jax.numpy as jnp
from jax import lax
from jax.sharding import PartitionSpec as P

TAPS = 7
GROUP = 16


def passed_along(array, axis, by):
    count = lax.axis_size(axis)
    pairs = [(i, i + by) for i in range(count) if 0 <= i + by < count]
    return lax.ppermute(array, axis, pairs)


def shards(q_proj, k_proj, v_proj, out_grad, out_weight, taps):
    tokens, channels = q_proj.shape
    rim_rows = TAPS - 1
    q_full = q_proj.astype(jnp.float32)
    k_full = k_proj.astype(jnp.float32)
    v_full = v_proj.astype(jnp.float32)
    spread = jnp.broadcast_to(taps[:, :, None], (TAPS, taps.shape[1], GROUP)).reshape(
        TAPS, channels
    )
    tail_rows = jnp.stack([k_proj[tokens - rim_rows :], v_proj[tokens - rim_rows :]])
    before = passed_along(tail_rows, "seq", 1)
    keys_wide = jnp.concatenate([before[0], k_proj], 0).astype(jnp.float32)
    values_wide = jnp.concatenate([before[1], v_proj], 0).astype(jnp.float32)
    product = keys_wide * values_wide
    filtered = jnp.zeros((tokens, channels), jnp.float32)
    for offset in range(TAPS):
        filtered = (
            filtered + spread[offset] * product[rim_rows - offset : rim_rows - offset + tokens]
        )
    gated = (q_full * filtered).astype(jnp.bfloat16)
    seq_count, mp_count = (lax.axis_size("seq"), lax.axis_size("mp"))
    cores = mp_count // seq_count
    pairs = [
        (t * mp_count + cores * z + c, z * mp_count + cores * t + c)
        for t in range(seq_count)
        for z in range(seq_count)
        for c in range(cores)
    ]
    crossed = lax.ppermute(out_grad, ("seq", "mp"), pairs)
    tiles = lax.all_gather(crossed, "mp", axis=0)
    columns = (
        tiles.reshape(seq_count, cores, tokens, channels)
        .transpose(0, 2, 1, 3)
        .reshape(seq_count * tokens, cores * channels)
    )
    partial = lax.dot_general(
        columns, out_weight, (((1,), (1,)), ((), ())), preferred_element_type=jnp.float32
    )
    grad_gated = lax.psum_scatter(partial, "seq", scatter_dimension=0, tiled=True)
    grad_weight = lax.dot_general(
        lax.all_gather(gated, "seq", axis=0, tiled=True),
        columns,
        (((0,), (0,)), ((), ())),
        preferred_element_type=jnp.float32,
    )
    grad_q = (grad_gated * filtered).astype(jnp.bfloat16)
    grad_filtered = grad_gated * q_full
    following = passed_along(grad_filtered[:rim_rows], "seq", -1)
    grad_ext = jnp.concatenate([grad_filtered, following], 0)
    grad_product = jnp.zeros((tokens, channels), jnp.float32)
    for offset in range(TAPS):
        grad_product = grad_product + spread[offset] * grad_ext[offset : offset + tokens]
    grad_k = (grad_product * v_full).astype(jnp.bfloat16)
    grad_v = (grad_product * k_full).astype(jnp.bfloat16)
    filter_terms = jnp.stack(
        [
            jnp.sum(grad_filtered * product[rim_rows - offset : rim_rows - offset + tokens], 0)
            for offset in range(TAPS)
        ]
    )
    filter_local = filter_terms.reshape(TAPS, channels // GROUP, GROUP).sum(-1)
    grad_taps = lax.psum(filter_local, "seq")
    return (grad_q, grad_k, grad_v, grad_weight, grad_taps)


def solution(mesh):
    placed = (
        P("seq", "mp"),
        P("seq", "mp"),
        P("seq", "mp"),
        P("seq", "mp"),
        P("mp", "seq"),
        P(None, "mp"),
    )
    return jax.shard_map(
        shards,
        mesh=mesh,
        in_specs=placed,
        out_specs=(P("seq", "mp"), P("seq", "mp"), P("seq", "mp"), P("mp", "seq"), P(None, "mp")),
        check_vma=False,
    )
```

profile of v0, /device:TPU:32, one launch (start us, length us, event | category | flops | bytes accessed | tf_op | source)
XLA Modules:
  0.0 327.7 jit_solution(6569584320959466278)
XLA Ops:
  7.2 0.0 copy-start
  7.2 0.0 all-gather.6.cloned.1.call-start
  7.2 3.1 collective-permute-start
  10.3 12.5 %collective-permute-done = bf16[256,256]{1,0:T(8,128)(2,1)S(1)} collective-permute-done((bf16[256,256]{1,0:T(8,128)(2,1)}, bf16[256,256]{1,0:T(8,128)(2,1)S(1)}, u32[]{:S(2)}, u32[]{:S(2)}) %collective-permute-start) | collective-permute-done | bytes 131104 | tf_op jit(solution)/shard_map/ppermute | solution.py:44
  22.8 0.0 copy-start.5
  22.8 0.7 copy-done.5
  23.5 0.0 all-gather.6.cloned.1.call-update
  23.5 0.0 all-gather.4.cloned.1.call-start
  23.5 0.7 slice_bitcast_fusion.2
  24.3 1.3 collective-permute-start.1
  25.6 0.9 slice_bitcast_fusion.10
  26.5 0.1 broadcast_in_dim.44
  26.6 0.1 broadcast_in_dim.45
  26.7 0.1 broadcast_in_dim.42
  26.8 0.1 broadcast_in_dim.43
  26.8 0.1 broadcast_in_dim.40
  26.9 0.1 broadcast_in_dim.41
  27.0 0.1 broadcast_in_dim.38
  27.1 0.1 broadcast_in_dim.39
  27.1 0.1 broadcast_in_dim.36
  27.2 0.1 broadcast_in_dim.37
  27.3 0.1 broadcast_in_dim.34
  27.4 0.1 broadcast_in_dim.35
  27.4 0.1 broadcast_in_dim.32
  27.5 0.1 broadcast_in_dim.33
  27.6 0.0 collective-permute-done.1
  27.6 1.0 convert_multiply_fusion.2
  28.7 1.8 fusion
  30.5 0.0 all-gather.4.cloned.1.call-update
  30.5 0.0 reduce-scatter.2.cloned.1.call-start
  30.6 87.3 %all-gather.6.cloned.1.call-done = bf16[8192,256]{1,0:T(8,128)(2,1)} async-done(((bf16[256,256]{1,0:T(8,128)(2,1)}), bf16[8192,256]{1,0:T(8,128)(2,1)}) %all-gather.6.cloned.1.call-update) | async-done | bytes 4194320 | tf_op jit(solution)/shard_map/all_gather | solution.py:45
  117.8 8.0 %copy.12 = bf16[16,2,256,256]{2,0,3,1:T(8,128)(2,1)} copy(bf16[16,2,256,256]{3,2,1,0:T(8,128)(2,1)} %bitcast.36) | data formatting | bytes 8388608 | tf_op jit(solution)/shard_map/reshape | solution.py:47
  125.8 4.4 %copy.13 = bf16[64,8,16,256]{3,1,2,0:T(8,128)(2,1)S(1)} copy(bf16[64,8,16,256]{3,2,1,0:T(8,128)(2,1)} %bitcast.35) | data formatting | bytes 8388608
  130.2 0.0 copy-start.1
  130.2 2.0 copy-done.1
  132.2 0.0 copy-done
  132.2 3.2 fusion.19
  135.4 0.0 reduce-scatter.2.cloned.1.call-update
  135.4 0.0 copy-start.4
  135.4 0.0 copy-start.2
  135.4 0.0 copy-start.3
  135.5 43.0 %all-gather.4.cloned.1.call-done = bf16[4096,256]{1,0:T(8,128)(2,1)} async-done(((bf16[256,256]{1,0:T(8,128)(2,1)}), bf16[4096,256]{1,0:T(8,128)(2,1)}) %all-gather.4.cloned.1.call-update) | async-done | bytes 2097168 | tf_op jit(solution)/shard_map/all_gather | solution.py:56
  178.5 4.9 %fusion.20 = f32[256,512]{1,0:T(8,128)} fusion(bf16[4096,256]{1,0:T(8,128)(2,1)} %all-gather.4.cloned.1.call-done, bf16[4096,512]{0,1:T(8,128)(2,1)} %bitcast.34), kind=kOutput, calls=%fused_computation.61 | convolution fusion | flops 1073741824 | bytes 6815744 | tf_op jit(solution)/shard_map/dot_general | solution.py:55
  183.4 91.8 %reduce-scatter.2.cloned.1.call-done = f32[256,256]{1,0:T(8,128)} async-done(((f32[4096,256]{1,0:T(8,128)}), f32[256,256]{1,0:T(8,128)}) %reduce-scatter.2.cloned.1.call-update) | async-done | bytes 262160 | tf_op jit(solution)/shard_map/reduce_scatter | solution.py:54
  275.2 0.0 copy-done.4
  275.2 1.9 multiply_reduce_fusion
  277.1 1.3 collective-permute-start.2
  278.4 0.1 stack.36
  278.4 0.1 stack.37
  278.5 0.1 stack.38
  278.6 0.1 stack.39
  278.7 0.1 stack.40
  278.8 0.1 stack.41
  278.8 0.1 stack.42
  279.0 0.1 reduce_sum.79
  279.1 40.5 %psum.7 = f32[7,16]{1,0:T(8,128)} all-reduce(f32[7,16]{1,0:T(8,128)S(1)} %reduce_sum.79), channel_id=1, replica_groups=mesh['seq'=16,'mp'=32] {'seq'}, use_global_device_ids=true, to_apply=%region_9.0 | all-reduce | flops 112 | bytes 896 | tf_op jit(solution)/shard_map/psum | solution.py:77
  319.6 0.0 collective-permute-done.2
  319.6 0.0 copy-done.2
  319.6 0.9 multiply_convert_fusion
  320.5 0.0 copy-done.3
  320.5 0.7 multiply_convert_fusion.1
  (10 shorter events, 0.1 us)
Async XLA Ops:
  7.2 125.0 %copy-start = (bf16[256,512]{1,0:T(8,128)(2,1)S(1)}, bf16[256,512]{1,0:T(8,128)(2,1)}, u32[]{:S(2)}) copy-start(bf16[256,512]{1,0:T(8,128)(2,1)} %param.10) | copy-start | bytes 786436
  7.2 110.7 %all-gather.6.cloned.1.call-start = ((), (), s32[]{:S(2)}) async-start(), calls=%async_computation.3 | async-start | bytes 4325376 | tf_op jit(solution)/shard_map/all_gather | solution.py:45
  7.2 15.6 %collective-permute-start = (bf16[256,256]{1,0:T(8,128)(2,1)}, bf16[256,256]{1,0:T(8,128)(2,1)S(1)}, u32[]{:S(2)}, u32[]{:S(2)}) collective-permute-start(bf16[256,256]{1,0:T(8,128)(2,1)} %param.9), channel_id=1, source_target_pairs={{0,0},{1,1},{2,32},{3,33},{4,64},{5,65},{6,96},{7,97},{8,128},{9,1... | collective-permute-start | bytes 393224 | tf_op jit(solution)/shard_map/ppermute | solution.py:44
  22.8 0.7 copy-start.5
  23.5 155.0 %all-gather.4.cloned.1.call-start = ((), (), s32[]{:S(2)}) async-start(), calls=%async_computation.2 | async-start | bytes 2228224 | tf_op jit(solution)/shard_map/all_gather | solution.py:56
  24.3 3.3 %collective-permute-start.1 = (bf16[2,6,256]{2,1,0:T(8,128)(2,1)S(1)}, bf16[2,6,256]{2,1,0:T(8,128)(2,1)S(1)}, u32[]{:S(2)}, u32[]{:S(2)}) collective-permute-start(bf16[2,6,256]{2,1,0:T(8,128)(2,1)S(1)} %pad_maximum_fusion.1), channel_id=1, source_target_pairs={{0,32},{32,64},{64,96},{96,128},{128,160},{160,192},{192,224},{224... | collective-permute-start | bytes 18440 | tf_op jit(solution)/shard_map/ppermute | solution.py:13
  30.5 244.7 %reduce-scatter.2.cloned.1.call-start = ((), (), s32[]{:S(2)}) async-start(), calls=%async_computation.1 | async-start | bytes 4456448 | tf_op jit(solution)/shard_map/reduce_scatter | solution.py:54
  130.2 2.0 copy-start.1
  135.4 139.8 %copy-start.4 = (bf16[256,256]{1,0:T(8,128)(2,1)S(1)}, bf16[256,256]{1,0:T(8,128)(2,1)}, u32[]{:S(2)}) copy-start(bf16[256,256]{1,0:T(8,128)(2,1)} %param.6) | copy-start | bytes 393220
  135.4 184.1 %copy-start.2 = (bf16[256,256]{1,0:T(8,128)(2,1)S(1)}, bf16[256,256]{1,0:T(8,128)(2,1)}, u32[]{:S(2)}) copy-start(bf16[256,256]{1,0:T(8,128)(2,1)} %param.7) | copy-start | bytes 393220
  135.4 185.0 %copy-start.3 = (bf16[256,256]{1,0:T(8,128)(2,1)S(1)}, bf16[256,256]{1,0:T(8,128)(2,1)}, u32[]{:S(2)}) copy-start(bf16[256,256]{1,0:T(8,128)(2,1)} %param.8) | copy-start | bytes 393220
  277.1 42.5 %collective-permute-start.2 = (f32[6,256]{1,0:T(8,128)S(1)}, f32[6,256]{1,0:T(8,128)S(1)}, u32[]{:S(2)}, u32[]{:S(2)}) collective-permute-start(f32[6,256]{1,0:T(8,128)S(1)} %slice.158), channel_id=1, source_target_pairs={{32,0},{64,32},{96,64},{128,96},{160,128},{192,160},{224,192},{256... | collective-permute-start | bytes 18440 | tf_op jit(solution)/shard_map/ppermute | solution.py:13
Sparse Core Ops, SparseCore 0:
  23.6 94.1 all-gather.5
  121.4 57.0 all-gather.3
  182.7 92.4 reduce-scatter.1
where the time goes:
time: 328 us
  waiting for transfers between devices  235 us (72%)
  blocking collectives  40.5 us (12%)
  local copies, waits for them, and re-layouts  18.3 us (6%)
  between operations  13.9 us (4%)
  matrix products  8.15 us (2%)
  other arithmetic  6.39 us (2%)
  starting transfers between devices  5.76 us (2%)
    reduce_scatter x1, waiting for transfers between devices, shards(): lax.psum_scatter(partial, 'seq', scatter_dimension=0, tiled=True)  91.8 us
    all_gather x1, waiting for transfers between devices, shards(): tiles = lax.all_gather(crossed, 'mp', axis=0)  87.3 us
    all_gather x1, waiting for transfers between devices, shards(): lax.all_gather(gated, 'seq', axis=0, tiled=True)  43 us
    psum x1, blocking collectives, shards(): grad_taps = lax.psum(filter_local, 'seq')  40.5 us
    ppermute x1, waiting for transfers between devices, shards(): crossed = lax.ppermute(out_grad, ('seq', 'mp'), pairs)  12.5 us
    reshape x1, local copies, waits for them, and re-layouts, shards(): tiles.reshape(seq_count, cores, tokens, channels).transpose(0, 2, 1, 3)  7.96 us
    unnamed x19, local copies, waits for them, and re-layouts  7.08 us
  transfers between devices with their start and end apart: 6, of which 4 were waited for; matrix products, arithmetic and copies ran while one was open for 8% of the time, Pallas kernels for 0%

commit v1 on v0

--- a/solution.py
+++ b/solution.py
@@ -5,6 +5,11 @@
 
 TAPS = 7
 GROUP = 16
+
+
+def add_all(x, axis):
+    parts = lax.all_gather(x, axis)
+    return jnp.sum(parts, axis=0)
 
 
 def passed_along(array, axis, by):
@@ -74,7 +79,7 @@
         ]
     )
     filter_local = filter_terms.reshape(TAPS, channels // GROUP, GROUP).sum(-1)
-    grad_taps = lax.psum(filter_local, "seq")
+    grad_taps = add_all(filter_local, "seq")
     return (grad_q, grad_k, grad_v, grad_weight, grad_taps)
 
 

time: 328 us -> 313 us (0.954)
  blocking collectives: 40.5 us -> 25 us
    psum x1 -> x0, blocking collectives: 40.5 us -> none  [shards(): grad_taps = lax.psum(filter_local, 'seq')]
    all_gather x0 -> x1, blocking collectives: none -> 25 us  [add_all(): parts = lax.all_gather(x, axis)]
  transfers between devices with their start and end apart: 6 -> 6, of which waited for: 4 -> 4; matrix products, arithmetic and copies ran while one was open for 8% -> 9% of each run, Pallas kernels for 0% -> 0%
where the time goes in v1:
time: 313 us
  waiting for transfers between devices  235 us (75%)
  blocking collectives  25 us (8%)
  local copies, waits for them, and re-layouts  18.3 us (6%)
  between operations  13.9 us (4%)
  matrix products  8.16 us (3%)
  other arithmetic  7.01 us (2%)
  starting transfers between devices  5.76 us (2%)
    reduce_scatter x1, waiting for transfers between devices, shards(): lax.psum_scatter(partial, 'seq', scatter_dimension=0, tiled=True)  91.8 us
    all_gather x1, waiting for transfers between devices, shards(): tiles = lax.all_gather(crossed, 'mp', axis=0)  87.3 us
    all_gather x1, waiting for transfers between devices, shards(): lax.all_gather(gated, 'seq', axis=0, tiled=True)  43 us
    all_gather x1, blocking collectives, add_all(): parts = lax.all_gather(x, axis)  25 us
    ppermute x1, waiting for transfers between devices, shards(): crossed = lax.ppermute(out_grad, ('seq', 'mp'), pairs)  12.5 us
    reshape x1, local copies, waits for them, and re-layouts, shards(): tiles.reshape(seq_count, cores, tokens, channels).transpose(0, 2, 1, 3)  7.96 us
    unnamed x19, local copies, waits for them, and re-layouts  7.08 us
  transfers between devices with their start and end apart: 6, of which 4 were waited for; matrix products, arithmetic and copies ran while one was open for 9% of the time, Pallas kernels for 0%

profile of v1, /device:TPU:32, one launch (start us, length us, event | category | flops | bytes accessed | tf_op | source)
XLA Modules:
  0.0 312.9 jit_solution(5977201514872526966)
XLA Ops:
  7.2 0.0 copy-start
  7.2 0.0 all-gather.8.cloned.1.call-start
  7.2 3.1 collective-permute-start
  10.3 12.5 %collective-permute-done = bf16[256,256]{1,0:T(8,128)(2,1)S(1)} collective-permute-done((bf16[256,256]{1,0:T(8,128)(2,1)}, bf16[256,256]{1,0:T(8,128)(2,1)S(1)}, u32[]{:S(2)}, u32[]{:S(2)}) %collective-permute-start) | collective-permute-done | bytes 131104 | tf_op jit(solution)/shard_map/ppermute | solution.py:49
  22.8 0.0 copy-start.5
  22.8 0.7 copy-done.5
  23.5 0.0 all-gather.8.cloned.1.call-update
  23.5 0.0 all-gather.6.cloned.1.call-start
  23.5 0.7 slice_bitcast_fusion.2
  24.3 1.3 collective-permute-start.1
  25.6 0.9 slice_bitcast_fusion.10
  26.5 0.1 broadcast_in_dim.44
  26.6 0.1 broadcast_in_dim.45
  26.7 0.1 broadcast_in_dim.42
  26.8 0.1 broadcast_in_dim.43
  26.8 0.1 broadcast_in_dim.40
  26.9 0.1 broadcast_in_dim.41
  27.0 0.1 broadcast_in_dim.38
  27.1 0.1 broadcast_in_dim.39
  27.1 0.1 broadcast_in_dim.36
  27.2 0.1 broadcast_in_dim.37
  27.3 0.1 broadcast_in_dim.34
  27.4 0.1 broadcast_in_dim.35
  27.4 0.1 broadcast_in_dim.32
  27.5 0.1 broadcast_in_dim.33
  27.6 0.0 collective-permute-done.1
  27.6 1.0 convert_multiply_fusion.2
  28.7 1.8 fusion
  30.5 0.0 all-gather.6.cloned.1.call-update
  30.5 0.0 reduce-scatter.2.cloned.1.call-start
  30.6 87.3 %all-gather.8.cloned.1.call-done = bf16[8192,256]{1,0:T(8,128)(2,1)} async-done(((bf16[256,256]{1,0:T(8,128)(2,1)}), bf16[8192,256]{1,0:T(8,128)(2,1)}) %all-gather.8.cloned.1.call-update) | async-done | bytes 4194320 | tf_op jit(solution)/shard_map/all_gather | solution.py:50
  117.8 8.0 %copy.13 = bf16[16,2,256,256]{2,0,3,1:T(8,128)(2,1)} copy(bf16[16,2,256,256]{3,2,1,0:T(8,128)(2,1)} %bitcast.37) | data formatting | bytes 8388608 | tf_op jit(solution)/shard_map/reshape | solution.py:52
  125.8 4.4 %copy.14 = bf16[64,8,16,256]{3,1,2,0:T(8,128)(2,1)S(1)} copy(bf16[64,8,16,256]{3,2,1,0:T(8,128)(2,1)} %bitcast.36) | data formatting | bytes 8388608
  130.2 0.0 copy-start.1
  130.2 2.0 copy-done.1
  132.2 0.0 copy-done
  132.2 3.2 %fusion.19 = f32[4096,256]{1,0:T(8,128)} fusion(bf16[4096,512]{0,1:T(8,128)(2,1)S(1)} %bitcast.34, bf16[256,512]{1,0:T(8,128)(2,1)S(1)} %copy-done), kind=kOutput, calls=%fused_computation.60 | convolution fusion | flops 1073741824 | bytes 8650752 | tf_op jit(solution)/shard_map/dot_general | solution.py:56
  135.4 0.0 reduce-scatter.2.cloned.1.call-update
  135.4 0.0 copy-start.4
  135.4 0.0 copy-start.2
  135.5 0.0 copy-start.3
  135.5 43.0 %all-gather.6.cloned.1.call-done = bf16[4096,256]{1,0:T(8,128)(2,1)} async-done(((bf16[256,256]{1,0:T(8,128)(2,1)}), bf16[4096,256]{1,0:T(8,128)(2,1)}) %all-gather.6.cloned.1.call-update) | async-done | bytes 2097168 | tf_op jit(solution)/shard_map/all_gather | solution.py:61
  178.5 4.9 %fusion.20 = f32[256,512]{1,0:T(8,128)} fusion(bf16[4096,256]{1,0:T(8,128)(2,1)} %all-gather.6.cloned.1.call-done, bf16[4096,512]{0,1:T(8,128)(2,1)} %bitcast.35), kind=kOutput, calls=%fused_computation.61 | convolution fusion | flops 1073741824 | bytes 6815744 | tf_op jit(solution)/shard_map/dot_general | solution.py:60
  183.4 91.8 %reduce-scatter.2.cloned.1.call-done = f32[256,256]{1,0:T(8,128)} async-done(((f32[4096,256]{1,0:T(8,128)}), f32[256,256]{1,0:T(8,128)}) %reduce-scatter.2.cloned.1.call-update) | async-done | bytes 262160 | tf_op jit(solution)/shard_map/reduce_scatter | solution.py:59
  275.2 0.0 copy-done.4
  275.2 1.9 multiply_reduce_fusion
  277.1 1.3 collective-permute-start.2
  278.4 0.1 stack.36
  278.4 0.1 stack.37
  278.5 0.1 stack.38
  278.6 0.1 stack.39
  278.7 0.1 stack.40
  278.8 0.1 stack.41
  278.8 0.1 stack.42
  279.0 0.1 reduce_sum.88
  279.1 25.0 %all-gather.2 = f32[16,7,16]{2,1,0:T(8,128)S(1)} all-gather(f32[1,7,16]{2,1,0:T(8,128)S(1)} %bitcast.38), channel_id=3, replica_groups=mesh['seq'=16,'mp'=32] {'seq'}, dimensions={0}, use_global_device_ids=true | all-gather | bytes 7616 | tf_op jit(solution)/shard_map/all_gather | solution.py:11
  304.1 0.6 reduce_sum.89
  304.7 0.0 collective-permute-done.2
  304.7 0.0 copy-done.2
  304.7 0.9 multiply_convert_fusion
  305.6 0.0 copy-done.3
  305.6 0.7 multiply_convert_fusion.1
  (10 shorter events, 0.1 us)
Async XLA Ops:
  7.2 125.0 %copy-start = (bf16[256,512]{1,0:T(8,128)(2,1)S(1)}, bf16[256,512]{1,0:T(8,128)(2,1)}, u32[]{:S(2)}) copy-start(bf16[256,512]{1,0:T(8,128)(2,1)} %param.10) | copy-start | bytes 786436
  7.2 110.7 %all-gather.8.cloned.1.call-start = ((), (), s32[]{:S(2)}) async-start(), calls=%async_computation.3 | async-start | bytes 4325376 | tf_op jit(solution)/shard_map/all_gather | solution.py:50
  7.2 15.6 %collective-permute-start = (bf16[256,256]{1,0:T(8,128)(2,1)}, bf16[256,256]{1,0:T(8,128)(2,1)S(1)}, u32[]{:S(2)}, u32[]{:S(2)}) collective-permute-start(bf16[256,256]{1,0:T(8,128)(2,1)} %param.9), channel_id=1, source_target_pairs={{0,0},{1,1},{2,32},{3,33},{4,64},{5,65},{6,96},{7,97},{8,128},{9,1... | collective-permute-start | bytes 393224 | tf_op jit(solution)/shard_map/ppermute | solution.py:49
  22.8 0.7 copy-start.5
  23.5 155.0 %all-gather.6.cloned.1.call-start = ((), (), s32[]{:S(2)}) async-start(), calls=%async_computation.2 | async-start | bytes 2228224 | tf_op jit(solution)/shard_map/all_gather | solution.py:61
  24.3 3.3 %collective-permute-start.1 = (bf16[2,6,256]{2,1,0:T(8,128)(2,1)S(1)}, bf16[2,6,256]{2,1,0:T(8,128)(2,1)S(1)}, u32[]{:S(2)}, u32[]{:S(2)}) collective-permute-start(bf16[2,6,256]{2,1,0:T(8,128)(2,1)S(1)} %pad_maximum_fusion.1), channel_id=1, source_target_pairs={{0,32},{32,64},{64,96},{96,128},{128,160},{160,192},{192,224},{224... | collective-permute-start | bytes 18440 | tf_op jit(solution)/shard_map/ppermute | solution.py:18
  30.5 244.7 %reduce-scatter.2.cloned.1.call-start = ((), (), s32[]{:S(2)}) async-start(), calls=%async_computation.1 | async-start | bytes 4456448 | tf_op jit(solution)/shard_map/reduce_scatter | solution.py:59
  130.2 2.0 copy-start.1
  135.4 139.8 %copy-start.4 = (bf16[256,256]{1,0:T(8,128)(2,1)S(1)}, bf16[256,256]{1,0:T(8,128)(2,1)}, u32[]{:S(2)}) copy-start(bf16[256,256]{1,0:T(8,128)(2,1)} %param.6) | copy-start | bytes 393220
  135.4 169.3 %copy-start.2 = (bf16[256,256]{1,0:T(8,128)(2,1)S(1)}, bf16[256,256]{1,0:T(8,128)(2,1)}, u32[]{:S(2)}) copy-start(bf16[256,256]{1,0:T(8,128)(2,1)} %param.7) | copy-start | bytes 393220
  135.5 170.2 %copy-start.3 = (bf16[256,256]{1,0:T(8,128)(2,1)S(1)}, bf16[256,256]{1,0:T(8,128)(2,1)}, u32[]{:S(2)}) copy-start(bf16[256,256]{1,0:T(8,128)(2,1)} %param.8) | copy-start | bytes 393220
  277.1 27.7 %collective-permute-start.2 = (f32[6,256]{1,0:T(8,128)S(1)}, f32[6,256]{1,0:T(8,128)S(1)}, u32[]{:S(2)}, u32[]{:S(2)}) collective-permute-start(f32[6,256]{1,0:T(8,128)S(1)} %slice.158), channel_id=1, source_target_pairs={{32,0},{64,32},{96,64},{128,96},{160,128},{192,160},{224,192},{256... | collective-permute-start | bytes 18440 | tf_op jit(solution)/shard_map/ppermute | solution.py:18
Sparse Core Ops, SparseCore 0:
  23.6 94.1 all-gather.7
  121.4 57.0 all-gather.5
  182.7 92.4 reduce-scatter.1
